TPU v7x, 256 devices: a whole 4x4x8 slice. The times are simulated.
256 devices in a mesh: seq: 32 (over z, y_lo, core), fsdp: 8 (over x, y_hi).
Axes of the slice: x: 4, y: 4 (y_hi: 2, y_lo: 2; y = y_hi * 2 + y_lo), z: 8, core: 2. Of those that a mesh axis runs over, the one named last changes fastest.
Arguments:
- inputs: bfloat16 [16, 4096, 1536], P('fsdp', 'seq'), may hold values from -6 to 6
- gain: float32 [1536], replicated, may hold values from 0.1 to 1.9
- param: bfloat16 [1536, 3, 1536], P('fsdp'), may hold values from -6 to 6
- cotangent: bfloat16 [16, 4096, 1536], P('fsdp', 'seq'), may hold values from -12 to 12
- noise: bfloat16 [1536, 3, 1536], P('fsdp'), may hold values from -6 to 6
Outputs:
- outputs: bfloat16 [16, 4096, 1536], P('fsdp', 'seq')
- new_param: bfloat16 [1536, 3, 1536], P('fsdp')
All inputs are finite; a program needn't handle non-finite values.
Results may differ from a plain program's by a relative error of at most 0.012.
Values may be sent and summed in bfloat16 or wider, within the bound.
No kernel may reach another device: no remote copies, remote signals or barrier semaphores. Data moves between devices by JAX's collectives and lax.ppermute only.
A program may use at most 128 MiB of HBM per device.

v0:
```python
import math
import jax
import jax.numpy as jnp
from jax import lax
from jax.sharding import PartitionSpec as P

DILATION_STEP = 16


def padded(x, sides, width):
    for axis, dim in sides:
        count, length = (lax.axis_size(axis), x.shape[dim])
        up = [(i, (i + 1) % count) for i in range(count - 1)]
        down = [(j, i) for i, j in up]
        last = lax.slice_in_dim(x, length - width, length, axis=dim)
        first = lax.slice_in_dim(x, 0, width, axis=dim)
        before = lax.ppermute(last, axis, up)
        after = lax.ppermute(first, axis, down)
        x = jnp.concatenate([before, x, after], axis=dim)
    return x


def normalise(values, gain):
    floats = values.astype(jnp.float32)
    factor = lax.rsqrt(jnp.mean(floats * floats, axis=-1, keepdims=True) + 1e-06)
    return jax.nn.gelu(floats * factor * gain).astype(jnp.bfloat16)


def convolve(source_rows, kernel, scale):
    span_length = source_rows.shape[1] - 2 * DILATION_STEP
    total = jnp.zeros((source_rows.shape[0], span_length, kernel.shape[0]), jnp.float32)
    for kernel_tap in range(3):
        input_window = source_rows[
            :, kernel_tap * DILATION_STEP : kernel_tap * DILATION_STEP + span_length, :
        ]
        total = total + lax.dot_general(
            input_window,
            kernel[:, kernel_tap, :],
            (((2,), (1,)), ((), ())),
            preferred_element_type=jnp.float32,
        )
    return total * scale


def shards(inputs, gain, param, cotangent, noise):
    seqs, span_length, width = inputs.shape
    scale = 1.0 / math.sqrt(3.0 * width)
    total_rows = seqs * lax.axis_size("fsdp") * span_length * lax.axis_size("seq")
    eta = math.sqrt(3.0 * width / total_rows)
    hidden_state = normalise(inputs, gain)
    padded_input = padded(hidden_state, (("seq", 1),), DILATION_STEP)
    mixed = convolve(padded_input, lax.all_gather(param, "fsdp", axis=0, tiled=True), scale)
    taps = []
    for kernel_tap in range(3):
        input_window = padded_input[
            :, kernel_tap * DILATION_STEP : kernel_tap * DILATION_STEP + span_length, :
        ]
        taps.append(
            lax.dot_general(
                cotangent,
                input_window,
                (((0, 1), (0, 1)), ((), ())),
                preferred_element_type=jnp.float32,
            )
        )
    term = (jnp.stack(taps, axis=1) * scale).astype(jnp.bfloat16)
    term = lax.optimization_barrier(term)
    share = lax.psum_scatter(
        term.astype(jnp.float32).astype(jnp.bfloat16), "fsdp", scatter_dimension=0, tiled=True
    ).astype(jnp.float32)
    seq_share = lax.psum_scatter(share, "seq", scatter_dimension=0, tiled=True)
    piece_rows = seq_share.shape[0]
    offset = lax.axis_index("seq") * piece_rows
    own_param = lax.dynamic_slice_in_dim(param, offset, piece_rows, 0)
    own_noise = lax.dynamic_slice_in_dim(noise, offset, piece_rows, 0)
    updated = (
        own_param.astype(jnp.float32)
        - eta * seq_share
        + math.sqrt(2.0 * eta) * own_noise.astype(jnp.float32)
    )
    new_param = lax.all_gather(updated.astype(jnp.bfloat16), "seq", axis=0, tiled=True)
    outputs = (inputs.astype(jnp.float32) + mixed).astype(jnp.bfloat16)
    return (outputs, new_param)


def solution(mesh):
    placed = (
        P("fsdp", "seq", None),
        P(),
        P("fsdp", None, None),
        P("fsdp", "seq", None),
        P("fsdp", None, None),
    )
    return jax.shard_map(
        shards,
        mesh=mesh,
        in_specs=placed,
        out_specs=(P("fsdp", "seq", None), P("fsdp", None, None)),
        check_vma=False,
    )
```

profile of v0, /device:TPU:1, one launch (start us, length us, event | category | flops | bytes accessed | tf_op | source)
XLA Modules:
  0.0 720.0 jit_solution(8907818899789513406)
XLA Ops:
  7.2 0.0 copy-start
  7.2 0.0 copy-start.1
  7.2 0.0 reduce-scatter.4.cloned.1.call-start
  7.2 1.5 fusion.9
  8.8 1.8 fusion.13
  10.6 5.1 collective-permute-start.1
  15.8 1.9 collective-permute-start
  17.7 0.0 copy-done.1
  17.7 1.4 convolution_bitcast_fusion.1
  19.2 0.0 collective-permute-done.1
  19.2 1.4 convolution_bitcast_fusion
  20.6 0.0 collective-permute-done
  20.6 1.4 convolution_bitcast_fusion.2
  22.0 7.4 %fusion = bf16[1536,3,1536]{0,2,1:T(8,128)(2,1)} fusion(f32[1536,1,1536]{0,2,1:T(8,128)S(1)} %convolution_bitcast_fusion, f32[1536,1,1536]{0,2,1:T(8,128)S(1)} %convolution_bitcast_fusion.1, f32[1536,1,1536]{0,2,1:T(8,128)S(1)} %convolution_bitcast_fusion.2), kind=kLoop, calls=%fused_computation.1 | loop fusion | flops 28311552 | bytes 42467328 | tf_op jit(solution)/shard_map/convert_element_type | solution.py:66
  29.4 17.9 %copy.33 = bf16[1536,4608]{1,0:T(8,128)(2,1)} copy(bf16[1536,4608]{0,1:T(8,128)(2,1)} %bitcast.49) | data formatting | bytes 28311552
  47.3 0.0 reduce-scatter.4.cloned.1.call-update
  47.4 0.0 all-reduce.3.cloned.1.call-start
  47.4 174.2 %reduce-scatter.4.cloned.1.call-done = bf16[192,4608]{1,0:T(8,128)(2,1)} async-done(((bf16[1536,4608]{1,0:T(8,128)(2,1)}), bf16[192,4608]{1,0:T(8,128)(2,1)}) %reduce-scatter.4.cloned.1.call-update) | async-done | bytes 1769488
  221.6 4.0 copy.34
  225.5 4.0 copy.24
  229.6 5.2 copy.25
  234.7 0.0 all-reduce.3.cloned.1.call-update
  234.8 0.0 copy-start.3
  234.8 0.0 all-gather.3.cloned.1.call-start
  234.8 0.7 all-gather.3.cloned.1.call-update
  235.5 0.0 all-gather.5.cloned.1.call-start
  235.6 0.0 copy-done.3
  235.6 0.6 dynamic-slice
  236.8 0.9 constant_dynamic-slice_fusion.1
  237.8 0.0 copy-done
  237.8 236.0 %all-reduce.3.cloned.1.call-done = f32[192,3,1536]{2,1,0:T(4,128)} async-done(((f32[192,3,1536]{2,1,0:T(4,128)}), f32[192,3,1536]{2,1,0:T(4,128)}) %all-reduce.3.cloned.1.call-update) | async-done | bytes 3538960
  473.8 1.6 fusion.21
  475.5 0.0 all-gather.5.cloned.1.call-update
  475.5 168.2 %all-gather.3.cloned.1.call-done = bf16[1536,3,1536]{2,0,1:T(8,128)(2,1)} async-done(((bf16[192,3,1536]{2,0,1:T(8,128)(2,1)}), bf16[1536,3,1536]{2,0,1:T(8,128)(2,1)}) %all-gather.3.cloned.1.call-update) | async-done | bytes 14155792 | tf_op jit(solution)/shard_map/all_gather | solution.py:52
  643.8 3.7 fusion.1
  647.5 0.0 copy-start.2
  647.5 3.8 fusion.2
  651.3 0.0 copy-done.2
  651.4 4.8 fusion.8
  656.1 54.1 %all-gather.5.cloned.1.call-done = bf16[192,3,1536]{2,1,0:T(4,128)(2,1)} async-done(((bf16[6,3,1536]{2,1,0:T(4,128)(2,1)}), bf16[192,3,1536]{2,1,0:T(4,128)(2,1)}) %all-gather.5.cloned.1.call-update) | async-done | bytes 1769488 | tf_op jit(solution)/shard_map/all_gather | solution.py:81
  710.2 3.2 copy.27
  (3 shorter events, 0.1 us)
Async XLA Ops:
  7.2 230.6 %copy-start = (bf16[192,3,1536]{2,0,1:T(8,128)(2,1)S(1)}, bf16[192,3,1536]{2,0,1:T(8,128)(2,1)}, u32[]{:S(2)}) copy-start(bf16[192,3,1536]{2,0,1:T(8,128)(2,1)} %param.9) | copy-start | bytes 5308420
  7.2 10.6 %copy-start.1 = (bf16[2,128,1536]{2,1,0:T(8,128)(2,1)S(1)}, bf16[2,128,1536]{2,1,0:T(8,128)(2,1)}, u32[]{:S(2)}) copy-start(bf16[2,128,1536]{2,1,0:T(8,128)(2,1)} %param.8) | copy-start | bytes 2359300
  7.2 214.4 %reduce-scatter.4.cloned.1.call-start = ((), (), s32[]{:S(2)}) async-start(), calls=%async_computation.3 | async-start | bytes 15925248
  10.6 8.5 %collective-permute-start.1 = (bf16[2,16,1536]{2,1,0:T(8,128)(2,1)S(1)}, bf16[2,16,1536]{2,1,0:T(8,128)(2,1)S(1)}, u32[]{:S(2)}, u32[]{:S(2)}) collective-permute-start(bf16[2,16,1536]{2,1,0:T(8,128)(2,1)S(1)} %get-tuple-element.9), channel_id=1, source_target_pairs={{8,0},{16,8},{24,16},{32,24},{40,32},{48,40},{56,48},{64,56},{72,6... | collective-permute-start | bytes 294920 | tf_op jit(solution)/shard_map/ppermute | solution.py:18
  15.8 4.8 collective-permute-start
  47.4 426.5 %all-reduce.3.cloned.1.call-start = ((), (), s32[]{:S(2)}) async-start(), calls=%async_computation.4 | async-start | bytes 9437184
  234.8 0.8 copy-start.3
  234.8 409.0 %all-gather.3.cloned.1.call-start = ((), (), s32[]{:S(2)}) async-start(), calls=%async_computation.1 | async-start | bytes 15925248 | tf_op jit(solution)/shard_map/all_gather | solution.py:52
  235.5 474.7 %all-gather.5.cloned.1.call-start = ((), (), s32[]{:S(2)}) async-start(), calls=%async_computation.2 | async-start | bytes 2433024 | tf_op jit(solution)/shard_map/all_gather | solution.py:81
  647.5 3.8 copy-start.2
Sparse Core Ops, SparseCore 0:
  47.5 174.0 reduce-scatter.3
  234.9 238.9 all-reduce.2
  476.8 166.8 all-gather.2
  646.2 63.9 all-gather.4
where the time goes:
time: 721 us; the launch traced here: 720 us
  waiting for transfers between devices  633 us (88%)
  local copies, waits for them, and re-layouts  36 us (5%)
  matrix products  16.6 us (2%)
  between operations  14.6 us (2%)
  other arithmetic  12.4 us (2%)
  starting transfers between devices  7.23 us (1%)
    unnamed x6, waiting for transfers between devices  411 us
    all_gather x1, waiting for transfers between devices, shards(): lax.all_gather(param, 'fsdp', axis=0, tiled=True)  168 us
    all_gather x1, waiting for transfers between devices, shards(): lax.all_gather(updated.astype(jnp.bfloat16), 'seq', axis=0, tiled=True)  54.1 us
    unnamed x12, local copies, waits for them, and re-layouts  25.8 us
  transfers between devices with their start and end apart: 6, of which 4 were waited for; matrix products, arithmetic and copies ran while one was open for 3% of the time, Pallas kernels for 0%

commit v1 on v0

--- a/solution.py
+++ b/solution.py
@@ -78,7 +78,12 @@
         - eta * seq_share
         + math.sqrt(2.0 * eta) * own_noise.astype(jnp.float32)
     )
-    new_param = lax.all_gather(updated.astype(jnp.bfloat16), "seq", axis=0, tiled=True)
+    new_param = jnp.concatenate(
+        lax.all_to_all(
+            jnp.stack([updated.astype(jnp.bfloat16)] * lax.axis_size("seq")), "seq", 0, 0
+        ),
+        axis=0,
+    )
     outputs = (inputs.astype(jnp.float32) + mixed).astype(jnp.bfloat16)
     return (outputs, new_param)
 

time: 721 us -> 688 us (0.954)
  waiting for transfers between devices: 633 us -> 590 us
    all_gather x1 -> x0, waiting for transfers between devices: 54.1 us -> none  [shards(): lax.all_gather(updated.astype(jnp.bfloat16), 'seq', axis=0, tiled=True)]
    all_gather x1, waiting for transfers between devices: 168 us -> 178 us  [shards(): lax.all_gather(param, 'fsdp', axis=0, tiled=True)]
    unnamed x6 -> x5, waiting for transfers between devices: 411 us -> 412 us
  transfers between devices with their start and end apart: 6 -> 6, of which waited for: 4 -> 3; matrix products, arithmetic and copies ran while one was open for 3% -> 3% of each run, Pallas kernels for 0% -> 0%
where the time goes in v1:
time: 688 us; the launch traced here: 687 us
  waiting for transfers between devices  590 us (86%)
  local copies, waits for them, and re-layouts  39.6 us (6%)
  matrix products  16.6 us (2%)
  between operations  14.5 us (2%)
  starting transfers between devices  14.2 us (2%)
  other arithmetic  11.7 us (2%)
    unnamed x5, waiting for transfers between devices  412 us
    all_gather x1, waiting for transfers between devices, shards(): lax.all_gather(param, 'fsdp', axis=0, tiled=True)  178 us
    unnamed x12, local copies, waits for them, and re-layouts  24.3 us
  transfers between devices with their start and end apart: 6, of which 3 were waited for; matrix products, arithmetic and copies ran while one was open for 3% of the time, Pallas kernels for 0%

profile of v1, /device:TPU:1, one launch (start us, length us, event | category | flops | bytes accessed | tf_op | source)
XLA Modules:
  0.0 686.5 jit_solution(7450138931573164355)
XLA Ops:
  7.2 0.0 copy-start
  7.2 0.0 reduce-scatter.4.cloned.1.call-start
  7.2 1.4 fusion.9
  8.7 1.8 fusion.13
  10.5 5.1 collective-permute-start.1
  15.7 1.9 collective-permute-start
  17.6 0.0 copy-done
  17.6 1.4 convolution_bitcast_fusion.1
  19.1 0.0 collective-permute-done.1
  19.1 1.4 convolution_bitcast_fusion
  20.5 0.0 collective-permute-done
  20.5 1.4 convolution_bitcast_fusion.2
  21.9 7.4 %fusion = bf16[1536,3,1536]{0,2,1:T(8,128)(2,1)} fusion(f32[1536,1,1536]{0,2,1:T(8,128)S(1)} %convolution_bitcast_fusion, f32[1536,1,1536]{0,2,1:T(8,128)S(1)} %convolution_bitcast_fusion.1, f32[1536,1,1536]{0,2,1:T(8,128)S(1)} %convolution_bitcast_fusion.2), kind=kLoop, calls=%fused_computation.1 | loop fusion | flops 28311552 | bytes 42467328 | tf_op jit(solution)/shard_map/convert_element_type | solution.py:66
  29.3 18.7 %copy.39 = bf16[1536,4608]{1,0:T(8,128)(2,1)} copy(bf16[1536,4608]{0,1:T(8,128)(2,1)} %bitcast.51) | data formatting | bytes 28311552
  48.0 0.0 reduce-scatter.4.cloned.1.call-update
  48.1 0.0 all-reduce.3.cloned.1.call-start
  48.1 174.2 %reduce-scatter.4.cloned.1.call-done = bf16[192,4608]{1,0:T(8,128)(2,1)} async-done(((bf16[1536,4608]{1,0:T(8,128)(2,1)}), bf16[192,4608]{1,0:T(8,128)(2,1)}) %reduce-scatter.4.cloned.1.call-update) | async-done | bytes 1769488
  222.3 4.0 copy.40
  226.3 2.8 copy.30
  229.1 3.7 copy.31
  232.8 0.0 all-reduce.3.cloned.1.call-update
  232.8 0.0 copy-start.3
  232.8 0.0 all-gather.2.cloned.1.call-start
  232.9 0.7 all-gather.2.cloned.1.call-update
  233.6 0.0 copy-done.3
  233.6 0.6 dynamic-slice
  234.8 237.2 %all-reduce.3.cloned.1.call-done = f32[192,3,1536]{2,1,0:T(4,128)} async-done(((f32[192,3,1536]{2,1,0:T(4,128)}), f32[192,3,1536]{2,1,0:T(4,128)}) %all-reduce.3.cloned.1.call-update) | async-done | bytes 3538960
  472.0 0.9 constant_dynamic-slice_fusion
  472.9 1.1 fusion.21
  474.0 1.6 stack.14
  475.6 7.0 %all-to-all-start = ((bf16[32,6,3,1536]{3,1,2,0:T(8,128)(2,1)}), bf16[32,6,3,1536]{3,1,2,0:T(8,128)(2,1)}, u32[]{:S(2)}, u32[]{:S(2)}) async-start(bf16[32,6,3,1536]{3,1,2,0:T(8,128)(2,1)} %stack.14), calls=%async_computation | async-start | bytes 4718592 | tf_op jit(solution)/shard_map/all_to_all | solution.py:82
  482.6 177.8 %all-gather.2.cloned.1.call-done = bf16[1536,3,1536]{2,0,1:T(8,128)(2,1)} async-done(((bf16[192,3,1536]{2,0,1:T(8,128)(2,1)}), bf16[1536,3,1536]{2,0,1:T(8,128)(2,1)}) %all-gather.2.cloned.1.call-update) | async-done | bytes 14155792 | tf_op jit(solution)/shard_map/all_gather | solution.py:52
  660.4 3.7 fusion.1
  664.1 0.0 copy-start.2
  664.1 3.8 fusion.2
  668.0 0.0 copy-done.2
  668.0 4.8 fusion.8
  672.7 0.0 all-to-all-done
  672.7 0.0 copy-start.1
  672.7 3.4 copy.33
  676.1 3.8 reshape.18
  680.0 0.0 copy-done.1
  (2 shorter events, 0.0 us)
Async XLA Ops:
  7.2 10.5 %copy-start = (bf16[2,128,1536]{2,1,0:T(8,128)(2,1)S(1)}, bf16[2,128,1536]{2,1,0:T(8,128)(2,1)}, u32[]{:S(2)}) copy-start(bf16[2,128,1536]{2,1,0:T(8,128)(2,1)} %param.8) | copy-start | bytes 2359300
  7.2 215.1 %reduce-scatter.4.cloned.1.call-start = ((), (), s32[]{:S(2)}) async-start(), calls=%async_computation.3 | async-start | bytes 15925248
  10.5 8.5 %collective-permute-start.1 = (bf16[2,16,1536]{2,1,0:T(8,128)(2,1)S(1)}, bf16[2,16,1536]{2,1,0:T(8,128)(2,1)S(1)}, u32[]{:S(2)}, u32[]{:S(2)}) collective-permute-start(bf16[2,16,1536]{2,1,0:T(8,128)(2,1)S(1)} %get-tuple-element.3), channel_id=1, source_target_pairs={{8,0},{16,8},{24,16},{32,24},{40,32},{48,40},{56,48},{64,56},{72,6... | collective-permute-start | bytes 294920 | tf_op jit(solution)/shard_map/ppermute | solution.py:18
  15.7 4.8 collective-permute-start
  48.1 423.9 %all-reduce.3.cloned.1.call-start = ((), (), s32[]{:S(2)}) async-start(), calls=%async_computation.4 | async-start | bytes 9437184
  232.8 0.8 copy-start.3
  232.8 427.6 %all-gather.2.cloned.1.call-start = ((), (), s32[]{:S(2)}) async-start(), calls=%async_computation.2 | async-start | bytes 15925248 | tf_op jit(solution)/shard_map/all_gather | solution.py:52
  475.6 197.2 %all-to-all-start = ((bf16[32,6,3,1536]{3,1,2,0:T(8,128)(2,1)}), bf16[32,6,3,1536]{3,1,2,0:T(8,128)(2,1)}, u32[]{:S(2)}, u32[]{:S(2)}) async-start(bf16[32,6,3,1536]{3,1,2,0:T(8,128)(2,1)} %stack.14), calls=%async_computation | async-start | bytes 4718592 | tf_op jit(solution)/shard_map/all_to_all | solution.py:82
  664.1 3.8 copy-start.2
  672.7 7.2 %copy-start.1 = (bf16[2,128,1536]{2,1,0:T(8,128)(2,1)S(1)}, bf16[2,128,1536]{2,1,0:T(8,128)(2,1)}, u32[]{:S(2)}) copy-start(bf16[2,128,1536]{2,1,0:T(8,128)(2,1)} %param.8) | copy-start | bytes 2359300
Sparse Core Ops, SparseCore 0:
  48.2 174.0 reduce-scatter.3
  232.9 238.9 all-reduce.2
  474.9 185.3 all-gather.1
